TPU v7x, 32 devices: a whole 2x2x4 slice. The times are simulated.
32 devices in a mesh: groups: 2 (over y), ctx: 4 (over z), exp: 2 (over x), tp: 2 (over core).
Axes of the slice: x: 2, y: 2, z: 4, core: 2. Of those that a mesh axis runs over, the one named last changes fastest.
Arguments:
- queries: bfloat16 [4, 512, 20, 128], P(('groups', 'exp'), 'ctx', 'tp'), parts along dimension 0, may hold values from -9 to 9
- key_states: bfloat16 [4, 512, 4, 128], P(('groups', 'exp'), 'ctx', 'tp'), parts along dimension 0, may hold values from -9 to 9
- values: bfloat16 [4, 512, 4, 128], P(('groups', 'exp'), 'ctx', 'tp'), parts along dimension 0, may hold values from -6 to 6
- doc_ids: int32 [4, 512], P(('groups', 'exp'), 'ctx'), parts along dimension 0, may hold values from 0 to 3, never falling along the last dimension, each value on 1 to 256 neighbouring positions
- residual: bfloat16 [4, 512, 5120], P(('groups', 'exp'), ('ctx', 'tp')), parts along dimension 0, may hold values from -6 to 6
- out_proj: bfloat16 [2560, 5120], P('tp', 'ctx'), may hold values from -0.125 to 0.125
- norm_gain: bfloat16 [5120], replicated, may hold values from 0.5 to 1.5
- router: bfloat16 [5120, 64], P(None, 'exp'), may hold values from -0.078125 to 0.078125
- expert_ids: int32 [4, 512, 1], P(('groups', 'exp'), ('ctx', 'tp')), parts along dimension 0, may hold values from 0 to 63; in each aligned block of 64 rows (0 to 63, 64 to 127, ..., all dimensions but the last counted through in order) at most 2 rows name the same one
- keep_counts: int32 [128], P('groups'), parts along dimension 0, may hold values from 1 to 2
Outputs:
- expert_inputs: bfloat16 [32, 64, 2, 5120], P(('groups', 'ctx', 'tp'), 'exp'), parts along dimension 0
There are 2 independent parts, one for each index of `groups`. A program takes and returns all parts, laid end to end along the dimension named above; an argument that names none is the same for every part. Nothing has to cross between parts.
Inputs may be any that keep to these rules, and one draw needn't show every extreme that they name: `doc_ids`: doc ids never fall along a request; a document holds at most 256 tokens, and some document holds exactly that many. `expert_ids`: in each aligned block of 64 tokens (the rows of one device) no expert is named more than 2 times, and in some blocks one expert is named exactly 2 times.
All inputs are finite; a program needn't handle non-finite values.
Results may differ from a plain program's by a relative error of at most 0.013.
Values may be sent and summed in bfloat16 or wider, within the bound.
A program may use at most 64 MiB of HBM per device.

v0:
```python
import math
import jax
import jax.numpy as jnp
from jax import lax
from jax.sharding import PartitionSpec as P

CAP = 2
EPSILON = 1e-05


def on_device(
    queries,
    key_states,
    values,
    doc_ids,
    residual,
    out_proj,
    norm_gain,
    router,
    expert_ids,
    keep_counts,
):
    tokens_here = queries.shape[1]
    heads_here = queries.shape[2]
    head_size = queries.shape[3]
    groups_here = key_states.shape[2]
    mixing_ratio = heads_here // groups_here
    ctx_count = lax.axis_size("ctx")
    pair_count = lax.axis_size("tp")
    part_rows = tokens_here // pair_count
    first_token = lax.axis_index("ctx") * tokens_here
    scale = 1.0 / math.sqrt(head_size)
    query_rows = (
        queries[0].reshape(tokens_here, groups_here, mixing_ratio, head_size).transpose(1, 0, 2, 3)
    )
    query_rows = query_rows.reshape(groups_here, tokens_here * mixing_ratio, head_size)
    query_place = (
        first_token
        + lax.broadcasted_iota(jnp.int32, (tokens_here * mixing_ratio,), 0) // mixing_ratio
    )
    query_docs = jnp.repeat(doc_ids[0], mixing_ratio)

    def update(running, key_block, value_block, doc_block, key_first):
        highest, totals, accum = running
        scores = (
            jnp.einsum("gqd,kgd->gqk", query_rows, key_block, preferred_element_type=jnp.float32)
            * scale
        )
        key_place = key_first + lax.broadcasted_iota(jnp.int32, (key_block.shape[0],), 0)
        allowed = (key_place[None, :] <= query_place[:, None]) & (
            doc_block[None, :] == query_docs[:, None]
        )
        masked = jnp.where(allowed[None], scores, -1e30)
        new_highest = jnp.maximum(highest, jnp.max(masked, axis=2))
        weights = jnp.where(allowed[None], jnp.exp(scores - new_highest[..., None]), 0.0)
        factor = jnp.exp(highest - new_highest)
        totals = totals * factor + jnp.sum(weights, axis=2)
        accum = accum * factor[..., None] + jnp.einsum(
            "gqk,kgd->gqd",
            weights.astype(jnp.bfloat16),
            value_block,
            preferred_element_type=jnp.float32,
        )
        return (new_highest, totals, accum)

    start_state = (
        jnp.full((groups_here, tokens_here * mixing_ratio), -1e30, jnp.float32),
        jnp.zeros((groups_here, tokens_here * mixing_ratio), jnp.float32),
        jnp.zeros((groups_here, tokens_here * mixing_ratio, head_size), jnp.float32),
    )
    key_piece = lax.all_gather(key_states, "ctx", axis=1, tiled=True)
    value_piece = lax.all_gather(values, "ctx", axis=1, tiled=True)
    doc_piece = lax.all_gather(doc_ids, "ctx", axis=1, tiled=True)
    piece_rows = key_piece.shape[1]
    block_rows = math.gcd(piece_rows, 512)

    def step(block_number, inner):
        block_offset = block_number * block_rows
        key_block = lax.dynamic_slice_in_dim(key_piece[0], block_offset, block_rows, 0)
        value_block = lax.dynamic_slice_in_dim(value_piece[0], block_offset, block_rows, 0)
        doc_block = lax.dynamic_slice_in_dim(doc_piece[0], block_offset, block_rows, 0)
        return update(inner, key_block, value_block, doc_block, block_offset)

    highest, totals, accum = lax.fori_loop(0, piece_rows // block_rows, step, start_state)
    blended_output = (accum / totals[..., None]).astype(jnp.bfloat16)
    blended_output = blended_output.reshape(
        groups_here, tokens_here, mixing_ratio, head_size
    ).transpose(1, 0, 2, 3)
    attn_rows = blended_output.reshape(pair_count, part_rows, heads_here * head_size)
    columns = out_proj.shape[1]
    gathered = lax.all_gather(attn_rows, "ctx", axis=1, tiled=True)
    gathered = gathered.reshape(pair_count * ctx_count * part_rows, heads_here * head_size)
    own_columns = lax.psum_scatter(
        jnp.dot(gathered, out_proj, preferred_element_type=jnp.float32).astype(jnp.bfloat16),
        "tp",
        scatter_dimension=0,
        tiled=True,
    ).astype(jnp.float32)
    own_columns = own_columns.reshape(ctx_count, part_rows, columns)
    projected = (
        lax.all_to_all(
            own_columns.astype(jnp.bfloat16), "ctx", split_axis=0, concat_axis=2, tiled=True
        )
        .astype(own_columns.dtype)
        .reshape(part_rows, columns * ctx_count)
    )
    hidden = residual[0].astype(jnp.float32) + projected
    power = jnp.mean(hidden * hidden, axis=1, keepdims=True)
    normed = (hidden * lax.rsqrt(power + EPSILON) * norm_gain.astype(jnp.float32)).astype(
        jnp.bfloat16
    )
    expert_count = keep_counts.shape[0]
    chosen = expert_ids[0, :, 0]
    onehot = (
        chosen[:, None] == lax.broadcasted_iota(jnp.int32, (part_rows, expert_count), 1)
    ).astype(jnp.float32)
    lower = (
        lax.broadcasted_iota(jnp.int32, (part_rows, part_rows), 0)
        > lax.broadcasted_iota(jnp.int32, (part_rows, part_rows), 1)
    ).astype(jnp.float32)
    earlier = jnp.dot(lower, onehot, preferred_element_type=jnp.float32)
    ranking = jnp.sum(onehot * earlier, axis=1)
    limits = jnp.sum(onehot * keep_counts.astype(jnp.float32)[None, :], axis=1)
    kept = ranking < limits
    target = chosen.astype(jnp.float32) * CAP + ranking
    slot_iota = lax.broadcasted_iota(jnp.int32, (expert_count * CAP, part_rows), 0).astype(
        jnp.float32
    )
    table = (slot_iota == target[None, :]) & kept[None, :]
    outgoing = jnp.dot(
        table.astype(jnp.bfloat16), normed, preferred_element_type=jnp.float32
    ).astype(jnp.bfloat16)
    exp_count = lax.axis_size("exp")
    outgoing = outgoing.reshape(exp_count, expert_count // exp_count, CAP, normed.shape[1])
    arrived = lax.all_to_all(outgoing, "exp", split_axis=0, concat_axis=0, tiled=True)
    logits = jnp.einsum("secd,de->sec", arrived, router, preferred_element_type=jnp.float32)
    return (arrived.astype(jnp.float32) * jax.nn.sigmoid(logits)[..., None]).astype(jnp.bfloat16)


def solution(mesh):
    placed = (
        P(("groups", "exp"), "ctx", "tp", None),
        P(("groups", "exp"), "ctx", "tp", None),
        P(("groups", "exp"), "ctx", "tp", None),
        P(("groups", "exp"), "ctx"),
        P(("groups", "exp"), ("ctx", "tp"), None),
        P("tp", "ctx"),
        P(),
        P(None, "exp"),
        P(("groups", "exp"), ("ctx", "tp"), None),
        P("groups"),
    )
    return jax.shard_map(
        on_device,
        mesh=mesh,
        in_specs=placed,
        out_specs=P(("groups", "ctx", "tp"), "exp", None, None),
        check_vma=False,
    )
```

profile of v0, /device:TPU:0, one launch (start us, length us, event | category | flops | bytes accessed | tf_op | source)
XLA Modules:
  0.0 172.3 jit_solution(3476322581073212627)
XLA Ops:
  6.5 12.9 %all_gather.14 = s32[1,512]{1,0:T(1,128)S(1)} all-gather(s32[1,128]{1,0:T(1,128)} %param.13), channel_id=1, replica_groups=mesh['groups'=2,'ctx'=4,'exp'=2,'tp'=2] {'ctx'}, dimensions={1}, use_global_device_ids=true | all-gather | bytes 2560 | tf_op jit(solution)/shard_map/all_gather | solution.py:73
  19.5 0.7 broadcast_in_dim.55
  20.4 0.9 copy.17
  21.3 13.9 %all_gather.16 = bf16[1,512,2,128]{3,1,2,0:T(8,128)(2,1)S(1)} all-gather(bf16[1,128,2,128]{3,1,2,0:T(8,128)(2,1)S(1)} %copy.17), channel_id=1, replica_groups=mesh['groups'=2,'ctx'=4,'exp'=2,'tp'=2] {'ctx'}, dimensions={1}, use_global_device_ids=true | all-gather | bytes 327680 | tf_op jit(solution)/shard_map/all_gather | solution.py:71
  35.2 1.3 copy.16
  36.8 0.7 select_reduce_fusion
  37.5 0.6 fusion
  38.3 14.1 %all_gather.17 = bf16[1,512,2,128]{3,1,2,0:T(8,128)(2,1)S(1)} all-gather(bf16[1,128,2,128]{3,1,2,0:T(8,128)(2,1)S(1)} %copy.19), channel_id=1, replica_groups=mesh['groups'=2,'ctx'=4,'exp'=2,'tp'=2] {'ctx'}, dimensions={1}, use_global_device_ids=true | all-gather | bytes 327680 | tf_op jit(solution)/shard_map/all_gather | solution.py:72
  52.5 1.2 fusion.18
  54.0 0.9 copy.22
  54.9 2.2 %reshape.135 = bf16[2,64,1280]{2,1,0:T(8,128)(2,1)} reshape(bf16[128,2,5,128]{3,2,1,0:T(8,128)(2,1)} %copy.22) | data formatting | bytes 655360 | tf_op jit(solution)/shard_map/reshape | solution.py:89
  57.1 30.9 %all-gather.2.cloned.1.call-done = bf16[2,256,1280]{2,1,0:T(8,128)(2,1)} async-done(((bf16[2,64,1280]{2,1,0:T(8,128)(2,1)}), bf16[2,256,1280]{2,1,0:T(8,128)(2,1)}) %all-gather.2.cloned.1.call-update) | async-done | bytes 1310736 | tf_op jit(solution)/shard_map/all_gather | solution.py:91
  88.1 4.2 %convolution_convert_fusion.1 = bf16[512,1280]{1,0:T(8,128)(2,1)} fusion(bf16[512,1280]{1,0:T(8,128)(2,1)} %bitcast.62, bf16[1280,1280]{1,0:T(8,128)(2,1)S(1)} %copy-done), kind=kOutput, calls=%fused_computation.1 | convolution fusion | flops 1678376960 | bytes 5898240 | tf_op jit(solution)/shard_map/dot_general | solution.py:94
  92.3 7.9 %reduce-scatter.2.cloned.1.call-done = bf16[256,1280]{1,0:T(8,128)(2,1)} async-done(((bf16[512,1280]{1,0:T(8,128)(2,1)}), bf16[256,1280]{1,0:T(8,128)(2,1)}) %reduce-scatter.2.cloned.1.call-update) | async-done | bytes 655376 | tf_op jit(solution)/shard_map/reduce_scatter | solution.py:93
  100.3 5.0 %all-to-all-start = ((bf16[4,64,1280]{2,1,0:T(8,128)(2,1)}), bf16[4,64,1280]{2,1,0:T(8,128)(2,1)}, u32[]{:S(2)}, u32[]{:S(2)}) async-start(bf16[4,64,1280]{2,1,0:T(8,128)(2,1)} %bitcast.55), calls=%async_computation.1 | async-start | bytes 1310720 | tf_op jit(solution)/shard_map/all_to_all | solution.py:101
  105.6 17.4 %all-to-all-done = bf16[4,64,1280]{2,1,0:T(8,128)(2,1)} async-done(((bf16[4,64,1280]{2,1,0:T(8,128)(2,1)}), bf16[4,64,1280]{2,1,0:T(8,128)(2,1)}, u32[]{:S(2)}, u32[]{:S(2)}) %all-to-all-start) | async-done | bytes 655392 | tf_op jit(solution)/shard_map/all_to_all | solution.py:101
  123.0 1.2 convert_bitcast_fusion
  124.2 0.8 copy.23
  125.3 0.8 copy-done.1
  126.4 1.6 convolution_convert_fusion
  128.0 3.9 %reshape.137 = bf16[2,32,2,5120]{3,2,1,0:T(2,128)(2,1)} reshape(bf16[128,5120]{1,0:T(8,128)(2,1)} %convolution_convert_fusion) | data formatting | bytes 2621440 | tf_op jit(solution)/shard_map/reshape | solution.py:134
  131.9 19.7 %all_to_all.14 = bf16[2,32,2,5120]{3,2,1,0:T(2,128)(2,1)S(1)} all-to-all(bf16[2,32,2,5120]{3,2,1,0:T(2,128)(2,1)} %reshape.137), channel_id=1, replica_groups=mesh['groups'=2,'ctx'=4,'exp'=2,'tp'=2] {'exp'}, dimensions={0} | all-to-all | bytes 2621440 | tf_op jit(solution)/shard_map/all_to_all | solution.py:135
  151.6 11.5 %fusion.9 = f32[32,1,2,2]{3,1,2,0:T(1,128)S(1)} fusion(bf16[2,32,2,5120]{3,2,1,0:T(2,128)(2,1)S(1)} %all_to_all.14, bf16[5120,32,1,1]{0,1,2,3:T(8,128)(2,1)S(1)} %bitcast.63), kind=kOutput, calls=%fused_computation.18 | convolution fusion | flops 1310720 | bytes 1638912 | tf_op jit(solution)/shard_map/secd,de->sec/dot_general | solution.py:136
  163.2 2.2 %multiply_convert_fusion = bf16[2,32,2,5120]{3,2,1,0:T(2,128)(2,1)} fusion(bf16[2,32,2,5120]{3,2,1,0:T(2,128)(2,1)S(1)} %all_to_all.14, f32[2,32,2]{2,1,0:T(8,128)S(1)} %fusion.34), kind=kLoop, calls=%fused_computation.2 | loop fusion | flops 1966080 | bytes 2621952 | tf_op jit(solution)/shard_map/convert_element_type | solution.py:137
  (34 shorter events, 2.0 us)
Async XLA Ops:
  6.5 81.5 %copy-start = (bf16[1280,1280]{1,0:T(8,128)(2,1)S(1)}, bf16[1280,1280]{1,0:T(8,128)(2,1)}, u32[]{:S(2)}) copy-start(bf16[1280,1280]{1,0:T(8,128)(2,1)} %param.15) | copy-start | bytes 9830404
  6.5 81.5 %all-gather.2.cloned.1.call-start = ((), (), s32[]{:S(2)}) async-start(), calls=%async_computation.3 | async-start | bytes 1638400 | tf_op jit(solution)/shard_map/all_gather | solution.py:91
  37.5 0.8 copy-start.2
  57.1 43.2 %reduce-scatter.2.cloned.1.call-start = ((), (), s32[]{:S(2)}) async-start(), calls=%async_computation.4 | async-start | bytes 1966080 | tf_op jit(solution)/shard_map/reduce_scatter | solution.py:93
  92.3 13.0 %copy-start.6 = (s32[64]{0:T(128)S(1)}, s32[64]{0:T(128)}, u32[]{:S(2)}) copy-start(s32[64]{0:T(128)} %param.19) | copy-start | bytes 772
  92.3 13.0 %copy-start.3 = (bf16[5120]{0:T(1024)(128)(2,1)S(1)}, bf16[5120]{0:T(1024)(128)(2,1)}, u32[]{:S(2)}) copy-start(bf16[5120]{0:T(1024)(128)(2,1)} %param.16) | copy-start | bytes 30724
  92.3 13.0 %copy-start.4 = (s32[1,64,1]{1,2,0:T(1,128)S(1)}, s32[1,64,1]{1,2,0:T(1,128)}, u32[]{:S(2)}) copy-start(s32[1,64,1]{1,2,0:T(1,128)} %param.18) | copy-start | bytes 772
  100.3 22.7 %all-to-all-start = ((bf16[4,64,1280]{2,1,0:T(8,128)(2,1)}), bf16[4,64,1280]{2,1,0:T(8,128)(2,1)}, u32[]{:S(2)}, u32[]{:S(2)}) async-start(bf16[4,64,1280]{2,1,0:T(8,128)(2,1)} %bitcast.55), calls=%async_computation.1 | async-start | bytes 1310720 | tf_op jit(solution)/shard_map/all_to_all | solution.py:101
  125.0 1.1 copy-start.1
  131.9 19.7 %copy-start.5 = (bf16[5120,32]{0,1:T(8,128)(2,1)S(1)}, bf16[5120,32]{0,1:T(8,128)(2,1)}, u32[]{:S(2)}) copy-start(bf16[5120,32]{0,1:T(8,128)(2,1)} %param.17) | copy-start | bytes 983044
Sparse Core Ops, SparseCore 0:
  57.2 30.8 all-gather.1
  92.4 7.7 reduce-scatter.1
where the time goes:
time: 173 us; the launch traced here: 172 us
  blocking collectives  60.6 us (35%)
  waiting for transfers between devices  56.3 us (33%)
  matrix products  19.5 us (11%)
  between operations  13.6 us (8%)
  local copies, waits for them, and re-layouts  12.5 us (7%)
  starting transfers between devices  5.02 us (3%)
  other arithmetic  4.83 us (3%)
    all_gather x1, waiting for transfers between devices, on_device(): gathered = lax.all_gather(attn_rows, 'ctx', axis=1, tiled=True)  30.9 us
    all_to_all x1, blocking collectives, on_device(): lax.all_to_all(outgoing, 'exp', split_axis=0, concat_axis=0, tiled=True)  19.7 us
    all_to_all x1, waiting for transfers between devices, on_device(): lax.all_to_all(own_columns.astype(jnp.bfloat16), 'ctx', split_axis=0, con...  17.4 us
    all_gather x1, blocking collectives, on_device(): value_piece = lax.all_gather(values, 'ctx', axis=1, tiled=True)  14.1 us
    all_gather x1, blocking collectives, on_device(): key_piece = lax.all_gather(key_states, 'ctx', axis=1, tiled=True)  13.9 us
    all_gather x1, blocking collectives, on_device(): doc_piece = lax.all_gather(doc_ids, 'ctx', axis=1, tiled=True)  12.9 us
    dot_general x1, matrix products, on_device(): jnp.einsum('secd,de->sec', arrived, router, preferred_element_type=jnp.fl...  11.5 us
    reduce_scatter x1, waiting for transfers between devices, on_device(): lax.psum_scatter(jnp.dot(gathered, out_proj, preferred_element_type=jnp.f...  7.95 us
  transfers between devices with their start and end apart: 3, of which 3 were waited for; matrix products, arithmetic and copies ran while one was open for 0% of the time, Pallas kernels for 0%

commit v1 on v0

--- a/solution.py
+++ b/solution.py
@@ -68,7 +68,25 @@
         jnp.zeros((groups_here, tokens_here * mixing_ratio), jnp.float32),
         jnp.zeros((groups_here, tokens_here * mixing_ratio, head_size), jnp.float32),
     )
-    key_piece = lax.all_gather(key_states, "ctx", axis=1, tiled=True)
+    devices, place, rows = (lax.axis_size("ctx"), lax.axis_index("ctx"), key_states.shape[1])
+    upward = [(i, (i + 1) % devices) for i in range(devices)]
+    backward = [(i, (i - 1) % devices) for i in range(devices)]
+    key_piece = jnp.zeros(
+        (*key_states.shape[:1], devices * rows, *key_states.shape[1 + 1 :]), key_states.dtype
+    )
+    key_piece = lax.dynamic_update_slice_in_dim(key_piece, key_states, place * rows, axis=1)
+    from_left = from_right = key_states
+    half = devices // 2
+    for k in range(1, half + 1):
+        from_left = lax.ppermute(from_left, "ctx", upward)
+        key_piece = lax.dynamic_update_slice_in_dim(
+            key_piece, from_left, (place - k) % devices * rows, axis=1
+        )
+        if k < devices - half:
+            from_right = lax.ppermute(from_right, "ctx", backward)
+            key_piece = lax.dynamic_update_slice_in_dim(
+                key_piece, from_right, (place + k) % devices * rows, axis=1
+            )
     value_piece = lax.all_gather(values, "ctx", axis=1, tiled=True)
     doc_piece = lax.all_gather(doc_ids, "ctx", axis=1, tiled=True)
     piece_rows = key_piece.shape[1]

time: 173 us -> 167 us (0.965)
  blocking collectives: 60.6 us -> 43.4 us
  waiting for transfers between devices: 56.3 us -> 62.1 us
  starting transfers between devices: 5.02 us -> 10.2 us
    all_gather x1 -> x0, blocking collectives: 13.9 us -> none  [on_device(): key_piece = lax.all_gather(key_states, 'ctx', axis=1, tiled=True)]
    ppermute x0 -> x3, waiting for transfers between devices: none -> 6.01 us  [the longest x2 6.01 us: on_device(): from_left = lax.ppermute(from_left, 'ctx', upward)]
    ppermute x0 -> x3, starting transfers between devices: none -> 5.2 us  [the longest x2 3.11 us: on_device(): from_left = lax.ppermute(from_left, 'ctx', upward)]
    all_gather x1, blocking collectives: 12.9 us -> 9.69 us  [on_device(): doc_piece = lax.all_gather(doc_ids, 'ctx', axis=1, tiled=True)]
  transfers between devices with their start and end apart: 3 -> 6, of which waited for: 3 -> 4; matrix products, arithmetic and copies ran while one was open for 0% -> 3% of each run, Pallas kernels for 0% -> 0%
where the time goes in v1:
time: 167 us
  waiting for transfers between devices  62.1 us (37%)
  blocking collectives  43.4 us (26%)
  matrix products  19.5 us (12%)
  between operations  13.6 us (8%)
  local copies, waits for them, and re-layouts  13.1 us (8%)
  starting transfers between devices  10.2 us (6%)
  other arithmetic  4.83 us (3%)
    all_gather x1, waiting for transfers between devices, on_device(): gathered = lax.all_gather(attn_rows, 'ctx', axis=1, tiled=True)  30.7 us
    all_to_all x1, blocking collectives, on_device(): lax.all_to_all(outgoing, 'exp', split_axis=0, concat_axis=0, tiled=True)  19.7 us
    all_to_all x1, waiting for transfers between devices, on_device(): lax.all_to_all(own_columns.astype(jnp.bfloat16), 'ctx', split_axis=0, con...  17.4 us
    all_gather x1, blocking collectives, on_device(): value_piece = lax.all_gather(values, 'ctx', axis=1, tiled=True)  14 us
    dot_general x1, matrix products, on_device(): jnp.einsum('secd,de->sec', arrived, router, preferred_element_type=jnp.fl...  11.5 us
    all_gather x1, blocking collectives, on_device(): doc_piece = lax.all_gather(doc_ids, 'ctx', axis=1, tiled=True)  9.69 us
    reduce_scatter x1, waiting for transfers between devices, on_device(): lax.psum_scatter(jnp.dot(gathered, out_proj, preferred_element_type=jnp.f...  7.95 us
    ppermute x2, waiting for transfers between devices, on_device(): from_left = lax.ppermute(from_left, 'ctx', upward)  6.01 us
  transfers between devices with their start and end apart: 6, of which 4 were waited for; matrix products, arithmetic and copies ran while one was open for 3% of the time, Pallas kernels for 0%

profile of v1, /device:TPU:0, one launch (start us, length us, event | category | flops | bytes accessed | tf_op | source)
XLA Modules:
  0.0 166.8 jit_solution(16915490235692272457)
XLA Ops:
  6.5 3.1 %collective-permute-start = (bf16[1,128,2,128]{3,2,1,0:T(2,128)(2,1)}, bf16[1,128,2,128]{3,2,1,0:T(2,128)(2,1)S(1)}, u32[]{:S(2)}, u32[]{:S(2)}) collective-permute-start(bf16[1,128,2,128]{3,2,1,0:T(2,128)(2,1)} %param.11), channel_id=1, source_target_pairs={{0,4},{4,8},{8,12},{12,0},{1,5},{5,9},{9,13},{13,1},{2,6},{6,10},{... | collective-permute-start | bytes 196616 | tf_op jit(solution)/shard_map/ppermute | solution.py:81
  9.6 2.1 %collective-permute-start.1 = (bf16[1,128,2,128]{3,2,1,0:T(2,128)(2,1)}, bf16[1,128,2,128]{3,2,1,0:T(2,128)(2,1)S(1)}, u32[]{:S(2)}, u32[]{:S(2)}) collective-permute-start(bf16[1,128,2,128]{3,2,1,0:T(2,128)(2,1)} %param.11), channel_id=1, source_target_pairs={{0,12},{4,0},{8,4},{12,8},{1,13},{5,1},{9,5},{13,9},{2,14},{6,2},{... | collective-permute-start | bytes 196616 | tf_op jit(solution)/shard_map/ppermute | solution.py:86
  11.7 9.7 %all_gather.11 = s32[1,512]{1,0:T(1,128)S(1)} all-gather(s32[1,128]{1,0:T(1,128)} %param.13), channel_id=1, replica_groups=mesh['groups'=2,'ctx'=4,'exp'=2,'tp'=2] {'ctx'}, dimensions={1}, use_global_device_ids=true | all-gather | bytes 2560 | tf_op jit(solution)/shard_map/all_gather | solution.py:91
  21.4 0.7 broadcast_in_dim.56
  22.3 2.0 %copy.23 = bf16[128,2,5,128]{3,1,2,0:T(2,128)(2,1)} copy(bf16[128,2,5,128]{3,0,2,1:T(8,128)(2,1)} %bitcast.76) | data formatting | bytes 655360 | tf_op jit(solution)/shard_map/reshape;squeeze | solution.py:34
  24.4 0.8 copy.25
  25.7 14.0 %all_gather.13 = bf16[1,512,2,128]{3,1,2,0:T(8,128)(2,1)S(1)} all-gather(bf16[1,128,2,128]{3,1,2,0:T(8,128)(2,1)S(1)} %copy.25), channel_id=1, replica_groups=mesh['groups'=2,'ctx'=4,'exp'=2,'tp'=2] {'ctx'}, dimensions={1}, use_global_device_ids=true | all-gather | bytes 327680 | tf_op jit(solution)/shard_map/all_gather | solution.py:90
  39.8 6.0 %collective-permute-done.2 = bf16[1,128,2,128]{3,2,1,0:T(2,128)(2,1)S(1)} collective-permute-done((bf16[1,128,2,128]{3,2,1,0:T(2,128)(2,1)S(1)}, bf16[1,128,2,128]{3,2,1,0:T(2,128)(2,1)S(1)}, u32[]{:S(2)}, u32[]{:S(2)}) %collective-permute-start.2) | collective-permute-done | bytes 65568 | tf_op jit(solution)/shard_map/ppermute | solution.py:81
  47.2 1.2 fusion.21
  48.8 0.9 copy.28
  49.7 2.1 %reshape.143 = bf16[2,64,1280]{2,1,0:T(8,128)(2,1)} reshape(bf16[128,2,5,128]{3,2,1,0:T(8,128)(2,1)} %copy.28) | data formatting | bytes 655360 | tf_op jit(solution)/shard_map/reshape | solution.py:107
  51.9 30.7 %all-gather.2.cloned.1.call-done = bf16[2,256,1280]{2,1,0:T(8,128)(2,1)} async-done(((bf16[2,64,1280]{2,1,0:T(8,128)(2,1)}), bf16[2,256,1280]{2,1,0:T(8,128)(2,1)}) %all-gather.2.cloned.1.call-update) | async-done | bytes 1310736 | tf_op jit(solution)/shard_map/all_gather | solution.py:109
  82.5 4.2 %convolution_convert_fusion.1 = bf16[512,1280]{1,0:T(8,128)(2,1)} fusion(bf16[512,1280]{1,0:T(8,128)(2,1)} %bitcast.86, bf16[1280,1280]{1,0:T(8,128)(2,1)S(1)} %copy-done), kind=kOutput, calls=%fused_computation.1 | convolution fusion | flops 1678376960 | bytes 5898240 | tf_op jit(solution)/shard_map/dot_general | solution.py:112
  86.8 7.9 %reduce-scatter.2.cloned.1.call-done = bf16[256,1280]{1,0:T(8,128)(2,1)} async-done(((bf16[512,1280]{1,0:T(8,128)(2,1)}), bf16[256,1280]{1,0:T(8,128)(2,1)}) %reduce-scatter.2.cloned.1.call-update) | async-done | bytes 655376 | tf_op jit(solution)/shard_map/reduce_scatter | solution.py:111
  94.8 5.0 %all-to-all-start = ((bf16[4,64,1280]{2,1,0:T(8,128)(2,1)}), bf16[4,64,1280]{2,1,0:T(8,128)(2,1)}, u32[]{:S(2)}, u32[]{:S(2)}) async-start(bf16[4,64,1280]{2,1,0:T(8,128)(2,1)} %bitcast.75), calls=%async_computation.1 | async-start | bytes 1310720 | tf_op jit(solution)/shard_map/all_to_all | solution.py:119
  100.0 17.4 %all-to-all-done = bf16[4,64,1280]{2,1,0:T(8,128)(2,1)} async-done(((bf16[4,64,1280]{2,1,0:T(8,128)(2,1)}), bf16[4,64,1280]{2,1,0:T(8,128)(2,1)}, u32[]{:S(2)}, u32[]{:S(2)}) %all-to-all-start) | async-done | bytes 655392 | tf_op jit(solution)/shard_map/all_to_all | solution.py:119
  117.5 1.2 convert_bitcast_fusion
  118.6 0.8 copy.29
  119.8 0.8 copy-done.1
  120.9 1.6 convolution_convert_fusion
  122.5 3.9 %reshape.145 = bf16[2,32,2,5120]{3,2,1,0:T(2,128)(2,1)} reshape(bf16[128,5120]{1,0:T(8,128)(2,1)} %convolution_convert_fusion) | data formatting | bytes 2621440 | tf_op jit(solution)/shard_map/reshape | solution.py:152
  126.4 19.7 %all_to_all.14 = bf16[2,32,2,5120]{3,2,1,0:T(2,128)(2,1)S(1)} all-to-all(bf16[2,32,2,5120]{3,2,1,0:T(2,128)(2,1)} %reshape.145), channel_id=1, replica_groups=mesh['groups'=2,'ctx'=4,'exp'=2,'tp'=2] {'exp'}, dimensions={0} | all-to-all | bytes 2621440 | tf_op jit(solution)/shard_map/all_to_all | solution.py:153
  146.1 11.5 %fusion.12 = f32[32,1,2,2]{3,1,2,0:T(1,128)S(1)} fusion(bf16[2,32,2,5120]{3,2,1,0:T(2,128)(2,1)S(1)} %all_to_all.14, bf16[5120,32,1,1]{0,1,2,3:T(8,128)(2,1)S(1)} %bitcast.87), kind=kOutput, calls=%fused_computation.21 | convolution fusion | flops 1310720 | bytes 1638912 | tf_op jit(solution)/shard_map/secd,de->sec/dot_general | solution.py:154
  157.7 2.2 %multiply_convert_fusion = bf16[2,32,2,5120]{3,2,1,0:T(2,128)(2,1)} fusion(bf16[2,32,2,5120]{3,2,1,0:T(2,128)(2,1)S(1)} %all_to_all.14, f32[2,32,2]{2,1,0:T(8,128)S(1)} %fusion.36), kind=kLoop, calls=%fused_computation.7 | loop fusion | flops 1966080 | bytes 2621952 | tf_op jit(solution)/shard_map/convert_element_type | solution.py:155
  (45 shorter events, 3.3 us)
Async XLA Ops:
  6.5 76.0 %copy-start = (bf16[1280,1280]{1,0:T(8,128)(2,1)S(1)}, bf16[1280,1280]{1,0:T(8,128)(2,1)}, u32[]{:S(2)}) copy-start(bf16[1280,1280]{1,0:T(8,128)(2,1)} %param.15) | copy-start | bytes 9830404
  6.5 18.8 %copy-start.3 = (bf16[1,128,2,128]{3,2,1,0:T(2,128)(2,1)S(1)}, bf16[1,128,2,128]{3,2,1,0:T(2,128)(2,1)}, u32[]{:S(2)}) copy-start(bf16[1,128,2,128]{3,2,1,0:T(2,128)(2,1)} %param.11) | copy-start | bytes 196612
  6.5 76.0 %all-gather.2.cloned.1.call-start = ((), (), s32[]{:S(2)}) async-start(), calls=%async_computation.3 | async-start | bytes 1638400 | tf_op jit(solution)/shard_map/all_gather | solution.py:109
  6.5 33.2 %collective-permute-start = (bf16[1,128,2,128]{3,2,1,0:T(2,128)(2,1)}, bf16[1,128,2,128]{3,2,1,0:T(2,128)(2,1)S(1)}, u32[]{:S(2)}, u32[]{:S(2)}) collective-permute-start(bf16[1,128,2,128]{3,2,1,0:T(2,128)(2,1)} %param.11), channel_id=1, source_target_pairs={{0,4},{4,8},{8,12},{12,0},{1,5},{5,9},{9,13},{13,1},{2,6},{6,10},{... | collective-permute-start | bytes 196616 | tf_op jit(solution)/shard_map/ppermute | solution.py:81
  9.6 30.2 %collective-permute-start.1 = (bf16[1,128,2,128]{3,2,1,0:T(2,128)(2,1)}, bf16[1,128,2,128]{3,2,1,0:T(2,128)(2,1)S(1)}, u32[]{:S(2)}, u32[]{:S(2)}) collective-permute-start(bf16[1,128,2,128]{3,2,1,0:T(2,128)(2,1)} %param.11), channel_id=1, source_target_pairs={{0,12},{4,0},{8,4},{12,8},{1,13},{5,1},{9,5},{13,9},{2,14},{6,2},{... | collective-permute-start | bytes 196616 | tf_op jit(solution)/shard_map/ppermute | solution.py:86
  25.2 20.6 %copy-start.2 = (bf16[128,2,5,128]{3,1,2,0:T(2,128)(2,1)S(1)}, bf16[128,2,5,128]{3,1,2,0:T(2,128)(2,1)}, u32[]{:S(2)}) copy-start(bf16[128,2,5,128]{3,1,2,0:T(2,128)(2,1)} %copy.23) | copy-start | bytes 983044
  39.7 6.1 %collective-permute-start.2 = (bf16[1,128,2,128]{3,2,1,0:T(2,128)(2,1)S(1)}, bf16[1,128,2,128]{3,2,1,0:T(2,128)(2,1)S(1)}, u32[]{:S(2)}, u32[]{:S(2)}) collective-permute-start(bf16[1,128,2,128]{3,2,1,0:T(2,128)(2,1)S(1)} %collective-permute-done), channel_id=1, source_target_pairs={{0,4},{4,8},{8,12},{12,0},{1,5},{5,9},{9,13},{13,1},{2,6},{6,10},{... | collective-permute-start | bytes 196616 | tf_op jit(solution)/shard_map/ppermute | solution.py:81
  51.8 42.9 %reduce-scatter.2.cloned.1.call-start = ((), (), s32[]{:S(2)}) async-start(), calls=%async_computation.4 | async-start | bytes 1966080 | tf_op jit(solution)/shard_map/reduce_scatter | solution.py:111
  86.8 13.0 %copy-start.7 = (s32[64]{0:T(128)S(1)}, s32[64]{0:T(128)}, u32[]{:S(2)}) copy-start(s32[64]{0:T(128)} %param.19) | copy-start | bytes 772
  86.8 13.0 %copy-start.4 = (bf16[5120]{0:T(1024)(128)(2,1)S(1)}, bf16[5120]{0:T(1024)(128)(2,1)}, u32[]{:S(2)}) copy-start(bf16[5120]{0:T(1024)(128)(2,1)} %param.16) | copy-start | bytes 30724
  86.8 13.0 %copy-start.5 = (s32[1,64,1]{1,2,0:T(1,128)S(1)}, s32[1,64,1]{1,2,0:T(1,128)}, u32[]{:S(2)}) copy-start(s32[1,64,1]{1,2,0:T(1,128)} %param.18) | copy-start | bytes 772
  94.8 22.7 %all-to-all-start = ((bf16[4,64,1280]{2,1,0:T(8,128)(2,1)}), bf16[4,64,1280]{2,1,0:T(8,128)(2,1)}, u32[]{:S(2)}, u32[]{:S(2)}) async-start(bf16[4,64,1280]{2,1,0:T(8,128)(2,1)} %bitcast.75), calls=%async_computation.1 | async-start | bytes 1310720 | tf_op jit(solution)/shard_map/all_to_all | solution.py:119
  119.5 1.1 copy-start.1
  126.4 19.7 %copy-start.6 = (bf16[5120,32]{0,1:T(8,128)(2,1)S(1)}, bf16[5120,32]{0,1:T(8,128)(2,1)}, u32[]{:S(2)}) copy-start(bf16[5120,32]{0,1:T(8,128)(2,1)} %param.17) | copy-start | bytes 983044
Sparse Core Ops, SparseCore 0:
  52.0 30.5 all-gather.1
  86.9 7.7 reduce-scatter.1
